TPU v7x, 32 devices: a whole 2x2x4 slice. The times are simulated.
32 devices in a mesh: clip: 2 (over x), tm: 2 (over core), space: 8 (over z, y).
Axes of the slice: x: 2, y: 2, z: 4, core: 2. Of those that a mesh axis runs over, the one named last changes fastest.
Arguments:
- queue_latents: float32 [16, 2, 16, 128], P(('clip', 'tm'), None, None, 'space'), parts along dimension 0, may hold values from -6 to 6
- fresh_noise: float32 [6, 2, 16, 128], P('clip', None, None, 'space'), parts along dimension 0, may hold values from -6 to 6
- slot_levels: int32 [16], P('clip'), parts along dimension 0, may hold values from 1 to 15, as said below
- level_table: float32 [16, 8, 1152], replicated, may hold values from -2.5 to 2.5
- embed_weight: float32 [16, 1152], replicated, may hold values from -1.5 to 1.5
- spatial_in: bfloat16 [1152, 1728], replicated, may hold values from -0.1875 to 0.1875
- spatial_out: bfloat16 [576, 1152], replicated, may hold values from -0.25 to 0.25
- temporal_in: bfloat16 [1152, 1728], replicated, may hold values from -0.1875 to 0.1875
- temporal_out: bfloat16 [576, 1152], replicated, may hold values from -0.25 to 0.25
- norm_gains: float32 [4, 72], replicated, may hold values from 0.1 to 1.9
- final_weight: float32 [1152, 16], replicated, may hold values from -0.1875 to 0.1875
Outputs:
- next_queue: float32 [16, 2, 16, 128], P(('clip', 'tm'), None, None, 'space'), parts along dimension 0
- denoised: float32 [16, 2, 16, 128], P(('clip', 'tm'), None, None, 'space'), parts along dimension 0
There are 2 independent parts, one for each index of `clip`. A program takes and returns all parts, laid end to end along the dimension named above; an argument that names none is the same for every part. Nothing has to cross between parts.
Inputs may be any that keep to these rules, and one draw needn't show every extreme that they name: `slot_levels`: strictly rising along the queue; neighbouring slots differ by 1 or 2; the last slot holds 15.
All inputs are finite; a program needn't handle non-finite values.
Results may differ from a plain program's by a relative error of at most 0.0023.
Values may be sent and summed in bfloat16 or wider, within the bound.
A program may use at most 128 MiB of HBM per device.

v0:
```python
import functools
import math

import jax
import jax.numpy as jnp
import numpy as np
from jax import lax
from jax.experimental import pallas as pl
from jax.experimental.pallas import tpu as pltpu
from jax.sharding import PartitionSpec as P

LEVELS = 16
LANES = 128
epsilon = 1e-06
highest = lax.Precision.HIGHEST
f32 = jnp.float32
bf16 = jnp.bfloat16


def sincos(count, width):
    half = width // 2
    rates = np.exp(-np.log(np.float32(10000.0)) * np.arange(half, dtype=np.float32) / np.float32(half))
    angles = np.arange(count, dtype=np.float32)[:, None] * rates[None, :].astype(np.float32)
    return np.concatenate([np.sin(angles), np.cos(angles)], axis=-1).astype(np.float32)


def layer_norm(values):
    centered = values - jnp.mean(values, axis=-1, keepdims=True)
    return centered * lax.rsqrt(jnp.mean(centered * centered, axis=-1, keepdims=True) + epsilon)


def head_norm(values, gain):
    return (
        values * lax.rsqrt(jnp.mean(values * values, axis=-1, keepdims=True) + epsilon) * gain
    ).astype(bf16)


def attention(projected, heads, size, query_gain, key_gain, mask):
    inner = heads * size
    mixed = []
    for head in range(heads):
        at = head * size
        queries = head_norm(projected[:, at : at + size], query_gain)
        keys = head_norm(projected[:, inner + at : inner + at + size], key_gain)
        values = projected[:, 2 * inner + at : 2 * inner + at + size].astype(bf16)
        scores = lax.dot_general(
            queries, keys, (((1,), (1,)), ((), ())), preferred_element_type=f32
        )
        weights = jnp.exp(scores * (1.0 / math.sqrt(size)))
        if mask is not None:
            weights = jnp.where(mask, weights, 0.0)
        totals = jnp.sum(weights, axis=-1, keepdims=True)
        total = jnp.dot(weights.astype(bf16), values, preferred_element_type=f32)
        mixed.append(total / totals)
    return jnp.concatenate(mixed, axis=-1)


def kernel(
    cfg,
    levels,
    start,
    noise,
    level_table,
    pos,
    embed,
    final_weight,
    gains,
    spatial_in_hbm,
    spatial_out_hbm,
    temporal_in_hbm,
    temporal_out_hbm,
    out,
    frame_latents,
    token_latents,
    mix_send,
    mix_recv,
    table,
    hidden,
    normed,
    ends,
    landed,
    spatial_in,
    spatial_out,
    temporal_in,
    temporal_out,
    weight_sem,
    start_send,
    start_recv,
    half_send,
    half_recv,
    mix_send_sem,
    mix_recv_sem,
    lat_send_sem,
    lat_recv_sem,
    end_send,
    end_recv,
):
    sections, shards, repeat = cfg["sections"], cfg["shards"], cfg["repeat"]
    slots, frames, steps = cfg["slots"], cfg["frames"], cfg["steps"]
    heads, size, piece = cfg["heads"], cfg["size"], cfg["piece"]
    width = embed.shape[1]
    group = sections * shards
    own_frames = slots * frames // sections
    rows = slots * frames * piece
    slab = frames * piece
    tokens = group * piece
    section, shard = lax.axis_index("tm"), lax.axis_index("space")
    item = section * shards + shard
    block = shard * sections + section
    frame = item // repeat
    own_slot = frame // frames

    weight_copies = [
        pltpu.make_async_copy(src, dst, weight_sem.at[n])
        for n, (src, dst) in enumerate(
            (
                (spatial_in_hbm, spatial_in),
                (spatial_out_hbm, spatial_out),
                (temporal_in_hbm, temporal_in),
                (temporal_out_hbm, temporal_out),
            )
        )
    ]
    for copy in weight_copies:
        copy.start()

    barrier = pltpu.get_barrier_semaphore()

    def greet(n, carry):
        other = lax.rem(item + n, group)
        pl.semaphore_signal(
            barrier,
            inc=1,
            device_id={"tm": other // shards, "space": lax.rem(other, shards)},
            device_id_type=pl.DeviceIdType.MESH,
        )
        return carry

    lax.fori_loop(1, group, greet, 0)
    pl.semaphore_wait(barrier, group - 1)

    def remote(src, dst, send, recv, to_section, to_shard):
        return pltpu.make_async_remote_copy(
            src_ref=src,
            dst_ref=dst,
            send_sem=send,
            recv_sem=recv,
            device_id={"tm": to_section, "space": to_shard},
            device_id_type=pl.DeviceIdType.MESH,
        )

    def start_copy(n):
        other = lax.rem(shard + n, shards)
        return remote(
            start.at[other // repeat],
            frame_latents.at[pl.ds(shard * sections, sections)],
            start_send.at[n],
            start_recv.at[n],
            section,
            other,
        )

    def half_copy(n):
        other = lax.rem(section + n, sections)
        return remote(
            start.at[:, other],
            token_latents.at[pl.ds(section * own_frames, own_frames)],
            half_send.at[n],
            half_recv.at[n],
            other,
            shard,
        )

    def mix_copy(n):
        other = lax.rem(block + n, group)
        return remote(
            mix_send.at[other],
            mix_recv.at[item],
            mix_send_sem.at[n],
            mix_recv_sem.at[n],
            lax.rem(other, sections),
            other // sections,
        )

    def lat_copy(n):
        other = lax.rem(item + n, group)
        return remote(
            token_latents.at[other // repeat],
            frame_latents.at[block],
            lat_send_sem.at[n],
            lat_recv_sem.at[n],
            other // shards,
            lax.rem(other, shards),
        )

    def end_copy(n):
        other = lax.rem(section + n, sections)
        return remote(
            ends.at[:, pl.ds(other * own_frames, own_frames)],
            landed.at[:, section],
            end_send.at[n],
            end_recv.at[n],
            other,
            shard,
        )

    def start_all(make, count):
        def one(n, carry):
            make(n).start()
            return carry

        lax.fori_loop(1, count, one, 0)

    def wait_all(make, count):
        def one(n, carry):
            make(n).wait()
            return carry

        lax.fori_loop(1, count, one, 0)

    start_all(start_copy, shards)
    start_all(half_copy, sections)
    frame_latents[pl.ds(shard * sections, sections)] = start[shard // repeat]
    token_latents[pl.ds(section * own_frames, own_frames)] = start[:, section]
    for slot in range(slots):
        table[slot] = level_table[levels[slot]]
    wait_all(start_copy, shards)
    wait_all(half_copy, sections)
    for copy in weight_copies:
        copy.wait()

    row_token = lax.rem(lax.broadcasted_iota(jnp.int32, (rows, rows), 0), piece)
    column_token = lax.rem(lax.broadcasted_iota(jnp.int32, (rows, rows), 1), piece)
    same_token = row_token == column_token

    def step_body(step, carry):
        whole = jnp.dot(
            frame_latents[...].reshape(tokens, LANES),
            embed[...],
            precision=highest,
            preferred_element_type=f32,
        )
        shift = table[own_slot, 0:1, :]
        scale = 1.0 + table[own_slot, 1:2, :]
        for at in range(0, tokens, slab):
            part = whole[at : at + slab] + pos[at : at + slab, :]
            normed[at : at + slab, :] = (layer_norm(part) * scale + shift).astype(bf16)
        projected = (
            jnp.dot(normed[0:tokens, :], spatial_in[...], preferred_element_type=f32)
            .astype(bf16)
            .astype(f32)
        )
        mixed = attention(
            projected, heads // repeat, size, gains[0:1, :], gains[1:2, :], None
        )
        mix_send[...] = mixed.reshape(group, piece, heads // repeat * size).astype(bf16)
        start_all(mix_copy, group)
        mix_recv[item] = mix_send[block]

        token_pos = pos[pl.ds(pl.multiple_of(block * piece, piece), piece), :]
        base = jnp.dot(
            token_latents[...].reshape(rows, LANES),
            embed[...],
            precision=highest,
            preferred_element_type=f32,
        )
        for n in range(slots * frames):
            hidden[n * piece : (n + 1) * piece, :] = (
                base[n * piece : (n + 1) * piece] + token_pos
            )
        wait_all(mix_copy, group)
        branch = None
        arrived = mix_recv[...].astype(f32).reshape(
            slots * frames, repeat, piece, heads // repeat * size
        )
        part_width = heads // repeat * size
        for n in range(repeat):
            part = jnp.dot(
                arrived[:, n].reshape(rows, part_width).astype(bf16),
                spatial_out[n * part_width : (n + 1) * part_width, :],
                preferred_element_type=f32,
            )
            branch = part if branch is None else branch + part
        for slot in range(slots):
            at = slot * slab
            frame_pos = jnp.concatenate(
                [
                    jnp.broadcast_to(
                        pos[slot * frames + n : slot * frames + n + 1, :], (piece, width)
                    )
                    for n in range(frames)
                ],
                axis=0,
            )
            part = (
                hidden[at : at + slab, :]
                + table[slot, 2:3, :] * branch[at : at + slab]
                + frame_pos
            )
            hidden[at : at + slab, :] = part
            normed[at : at + slab, :] = (
                layer_norm(part) * (1.0 + table[slot, 4:5, :]) + table[slot, 3:4, :]
            ).astype(bf16)
        projected = (
            jnp.dot(normed[0:rows, :], temporal_in[...], preferred_element_type=f32)
            .astype(bf16)
            .astype(f32)
        )
        mixed = attention(projected, heads, size, gains[2:3, :], gains[3:4, :], same_token)
        branch = jnp.dot(mixed.astype(bf16), temporal_out[...], preferred_element_type=f32)
        for slot in range(slots):
            at = slot * slab
            part = hidden[at : at + slab, :] + table[slot, 5:6, :] * branch[at : at + slab]
            hidden[at : at + slab, :] = (
                layer_norm(part) * (1.0 + table[slot, 7:8, :]) + table[slot, 6:7, :]
            )
        velocity = jnp.dot(
            hidden[...], final_weight[...], precision=highest, preferred_element_type=f32
        ).reshape(slots, frames, piece, LANES)
        before = jnp.float32(0.0)
        for slot in range(slots):
            time = (levels[slot].astype(f32) + 1.0) / LEVELS
            old = token_latents[slot * frames : (slot + 1) * frames]
            ends[1, slot * frames : (slot + 1) * frames] = old - time * velocity[slot]
            if slot > 0:
                token_latents[(slot - 1) * frames : slot * frames] = (
                    old - (time - before) * velocity[slot]
                )
            before = time
        token_latents[(slots - 1) * frames : slots * frames] = noise[step, :, section]

        @pl.when(step < steps - 1)
        def _():
            start_all(lat_copy, group)
            frame_latents[block] = token_latents[frame]
            wait_all(lat_copy, group)

        return carry

    lax.fori_loop(0, steps, step_body, 0)
    ends[0] = token_latents[...]
    start_all(end_copy, sections)
    landed[:, section] = ends[:, pl.ds(section * own_frames, own_frames)]
    wait_all(end_copy, sections)
    out[...] = landed[...]


def per_device(
    queue_latents,
    fresh_noise,
    slot_levels,
    level_table,
    embed_weight,
    spatial_in,
    spatial_out,
    temporal_in,
    temporal_out,
    norm_gains,
    final_weight,
):
    blocks, frames, channels, tokens = queue_latents.shape
    steps, slots = fresh_noise.shape[0], slot_levels.shape[0]
    sections, shards = lax.axis_size("tm"), lax.axis_size("space")
    width, size = embed_weight.shape[1], norm_gains.shape[1]
    inner = spatial_out.shape[0]
    heads = inner // size
    group = sections * shards
    repeat = group // (slots * frames)
    piece = tokens // sections
    own_frames = blocks * frames
    assert repeat * slots * frames == group and heads % repeat == 0
    assert piece * sections == tokens and own_frames * sections == slots * frames
    widen = ((0, 0),) * 3 + ((0, LANES - channels),)
    start = jnp.pad(jnp.transpose(queue_latents, (0, 1, 3, 2)), widen).reshape(
        own_frames, sections, piece, LANES
    )
    noise = jnp.pad(jnp.transpose(fresh_noise, (0, 1, 3, 2)), widen).reshape(
        steps, frames, sections, piece, LANES
    )
    embed = jnp.pad(embed_weight, ((0, LANES - channels), (0, 0)))
    final = jnp.pad(final_weight, ((0, 0), (0, LANES - channels)))
    part = inner // repeat
    if repeat > 1:
        which = lax.rem(lax.axis_index("space"), repeat)
        spatial_in = lax.dynamic_index_in_dim(
            spatial_in.reshape(width, 3, repeat, part), which, axis=2, keepdims=False
        ).reshape(width, 3 * part)
    rows = max(slots * frames * piece, group * piece)
    cfg = dict(
        sections=sections,
        shards=shards,
        repeat=repeat,
        slots=slots,
        frames=frames,
        steps=steps,
        heads=heads,
        size=size,
        piece=piece,
    )
    vmem, anywhere = pl.BlockSpec(memory_space=pltpu.VMEM), pl.BlockSpec(memory_space=pl.ANY)
    dma = pltpu.SemaphoreType.DMA
    out = pl.pallas_call(
        functools.partial(kernel, cfg),
        out_shape=jax.ShapeDtypeStruct((2, sections, own_frames, piece, LANES), f32),
        in_specs=[pl.BlockSpec(memory_space=pltpu.SMEM)] + [vmem] * 7 + [anywhere] * 4,
        out_specs=vmem,
        scratch_shapes=[
            pltpu.VMEM((group, piece, LANES), f32),
            pltpu.VMEM((slots * frames, piece, LANES), f32),
            pltpu.VMEM((group, piece, part), bf16),
            pltpu.VMEM((group, piece, part), bf16),
            pltpu.VMEM((slots, level_table.shape[1], width), f32),
            pltpu.VMEM((slots * frames * piece, width), f32),
            pltpu.VMEM((rows, width), bf16),
            pltpu.VMEM((2, slots * frames, piece, LANES), f32),
            pltpu.VMEM((2, sections, own_frames, piece, LANES), f32),
            pltpu.VMEM(spatial_in.shape, bf16),
            pltpu.VMEM(spatial_out.shape, bf16),
            pltpu.VMEM(temporal_in.shape, bf16),
            pltpu.VMEM(temporal_out.shape, bf16),
            dma((4,)),
            dma((shards,)),
            dma((shards,)),
            dma((sections,)),
            dma((sections,)),
            dma((group,)),
            dma((group,)),
            dma((group,)),
            dma((group,)),
            dma((sections,)),
            dma((sections,)),
        ],
        compiler_params=pltpu.CompilerParams(
            collective_id=0, has_side_effects=True, vmem_limit_bytes=60 * 1024 * 1024
        ),
    )(
        slot_levels,
        start,
        noise,
        level_table,
        jnp.asarray(sincos(max(group * piece, slots * frames), width)),
        embed,
        final,
        norm_gains,
        spatial_in,
        spatial_out,
        temporal_in,
        temporal_out,
    )
    ends = jnp.transpose(out[..., :channels], (0, 2, 4, 1, 3)).reshape(
        2, blocks, frames, channels, tokens
    )
    return (ends[0], ends[1])


def solution(mesh):
    own = P(("clip", "tm"), None, None, "space")
    return jax.shard_map(
        per_device,
        mesh=mesh,
        in_specs=(own, P("clip", None, None, "space"), P("clip")) + (P(),) * 8,
        out_specs=(own, own),
        check_vma=False,
    )
```

profile of v0, /device:TPU:0, one launch (start us, length us, event | category | flops | bytes accessed | tf_op | source)
XLA Modules:
  0.0 85.8 jit_solution(17704086077028183307)
XLA Ops:
  0.6 0.9 %copy.29 = f32[3,2,16,16]{3,2,1,0:T(8,128)S(1)} copy(f32[3,2,16,16]{2,3,1,0:T(8,128)} %bitcast.13) | data formatting | bytes 12288
  1.5 0.6 pad_bitcast_fusion.noise
  2.1 0.9 %copy.28 = f32[4,2,16,16]{3,2,1,0:T(8,128)S(1)} copy(f32[4,2,16,16]{2,3,1,0:T(8,128)} %bitcast.12) | data formatting | bytes 16384
  3.0 0.6 pad.16.clone
  3.7 1.8 %pad.18.embed = f32[128,1152]{1,0:T(8,128)} pad(f32[16,1152]{1,0:T(8,128)} %param.16, f32[]{:T(128)} %constant.4.clone.1), padding=0_112x0_0 | pad | bytes 663556 | tf_op jit(solution)/shard_map/jit(_pad)/pad | solution.py:380
  5.5 1.1 %copy.21 = f32[1152,16]{1,0:T(8,128)S(1)} copy(f32[1152,16]{0,1:T(8,128)} %param.22) | data formatting | bytes 147456 | tf_op args[10]
  6.6 1.0 %pad.19.final_weight = f32[1152,128]{1,0:T(8,128)} pad(f32[1152,16]{1,0:T(8,128)S(1)} %copy.21, f32[]{:T(128)} %constant.4.clone.1), padding=0_0x0_112 | pad | bytes 663556 | tf_op jit(solution)/shard_map/jit(_pad)/pad | solution.py:381
  7.6 6.4 %copy.22.spatial_in_hbm = bf16[1152,1728]{1,0:T(8,128)(2,1)} copy(bf16[1152,1728]{0,1:T(8,128)(2,1)} %param.17) | data formatting | bytes 7962624 | tf_op args[5]
  14.0 6.4 %copy.23.temporal_in_hbm = bf16[1152,1728]{1,0:T(8,128)(2,1)} copy(bf16[1152,1728]{0,1:T(8,128)(2,1)} %param.19) | data formatting | bytes 7962624 | tf_op args[7]
  20.4 63.0 %shard_map.131 = f32[2,2,8,8,128]{4,3,2,1,0:T(8,128)} custom-call(s32[8]{0:T(128)} %levels.1, f32[8,2,8,128]{3,2,1,0:T(8,128)} %bitcast.9, f32[3,2,2,8,128]{4,3,2,1,0:T(8,128)} %pad_bitcast_fusion.noise, f32[16,8,1152]{2,1,0:T(8,128)} %level_table.1, f32[128,1152]{1,0:T(8,128)} %constant.5.clone.pos, f32[128,1152]{1,0:T(8,128)} %pad.18.embed, ...), custom_call_target="tpu_custom_call" | custom-call | tf_op jit(solution)/shard_map/pallas_call | solution.py:402
  83.4 0.9 %slice_bitcast_fusion = f32[2,8,16,2,8]{2,4,1,3,0:T(8,128)S(1)} fusion(f32[2,2,8,8,128]{4,3,2,1,0:T(8,128)} %shard_map.131), kind=kLoop, calls=%fused_computation | loop fusion | bytes 32768 | tf_op jit(solution)/shard_map/transpose | solution.py:450
  84.4 0.7 copy.27
  85.1 0.7 copy.26
  (3 shorter events, 0.0 us)
where the time goes:
time: 86.4 us; the launch traced here: 85.8 us
  Pallas kernels  63 us (73%)
  local copies, waits for them, and re-layouts  22.2 us (26%)
    pallas_call x1, Pallas kernels, per_device(): pl.pallas_call(functools.partial(kernel, cfg), out_shape=jax.ShapeDtypeSt...  63 us
    unnamed x7, local copies, waits for them, and re-layouts  17.2 us
    pad x1, local copies, waits for them, and re-layouts, per_device(): embed = jnp.pad(embed_weight, ((0, LANES - channels), (0, 0)))  1.81 us

commit v1 on v0

--- a/solution.py
+++ b/solution.py
@@ -10,9 +10,7 @@
 from jax.sharding import PartitionSpec as P
 
 LEVELS = 16
-LANES = 128
 epsilon = 1e-06
-highest = lax.Precision.HIGHEST
 f32 = jnp.float32
 bf16 = jnp.bfloat16
 
@@ -35,24 +33,46 @@
     ).astype(bf16)
 
 
-def attention(projected, heads, size, query_gain, key_gain, mask):
+def split(values):
+    high = values.astype(bf16)
+    return high, (values - high.astype(f32)).astype(bf16)
+
+
+def heads_of(projected, heads, size, query_gain, key_gain):
     inner = heads * size
-    mixed = []
+    result = []
     for head in range(heads):
         at = head * size
-        queries = head_norm(projected[:, at : at + size], query_gain)
-        keys = head_norm(projected[:, inner + at : inner + at + size], key_gain)
-        values = projected[:, 2 * inner + at : 2 * inner + at + size].astype(bf16)
+        result.append(
+            (
+                head_norm(projected[:, at : at + size], query_gain),
+                head_norm(projected[:, inner + at : inner + at + size], key_gain),
+                projected[:, 2 * inner + at : 2 * inner + at + size].astype(bf16),
+            )
+        )
+    return result
+
+
+def attention(triples, first, count, mask):
+    mixed = []
+    for queries, keys, values in triples:
         scores = lax.dot_general(
-            queries, keys, (((1,), (1,)), ((), ())), preferred_element_type=f32
-        )
-        weights = jnp.exp(scores * (1.0 / math.sqrt(size)))
+            queries[first : first + count],
+            keys,
+            (((1,), (1,)), ((), ())),
+            preferred_element_type=f32,
+        )
+        weights = jnp.exp(scores * (1.0 / math.sqrt(values.shape[1])))
         if mask is not None:
             weights = jnp.where(mask, weights, 0.0)
         totals = jnp.sum(weights, axis=-1, keepdims=True)
         total = jnp.dot(weights.astype(bf16), values, preferred_element_type=f32)
         mixed.append(total / totals)
     return jnp.concatenate(mixed, axis=-1)
+
+
+def nt_dot(left, right):
+    return lax.dot_general(left, right, (((1,), (1,)), ((), ())), preferred_element_type=f32)
 
 
 def kernel(
@@ -77,6 +97,9 @@
     table,
     hidden,
     normed,
+    finals,
+    embed_halves,
+    final_halves,
     ends,
     landed,
     spatial_in,
@@ -98,7 +121,8 @@
     sections, shards, repeat = cfg["sections"], cfg["shards"], cfg["repeat"]
     slots, frames, steps = cfg["slots"], cfg["frames"], cfg["steps"]
     heads, size, piece = cfg["heads"], cfg["size"], cfg["piece"]
-    width = embed.shape[1]
+    channels, width = embed.shape
+    lanes = piece * channels
     group = sections * shards
     own_frames = slots * frames // sections
     rows = slots * frames * piece
@@ -106,7 +130,6 @@
     tokens = group * piece
     section, shard = lax.axis_index("tm"), lax.axis_index("space")
     item = section * shards + shard
-    block = shard * sections + section
     frame = item // repeat
     own_slot = frame // frames
 
@@ -153,7 +176,7 @@
         other = lax.rem(shard + n, shards)
         return remote(
             start.at[other // repeat],
-            frame_latents.at[pl.ds(shard * sections, sections)],
+            frame_latents.at[:, shard],
             start_send.at[n],
             start_recv.at[n],
             section,
@@ -172,21 +195,21 @@
         )
 
     def mix_copy(n):
-        other = lax.rem(block + n, group)
+        other = lax.rem(item + n, group)
         return remote(
             mix_send.at[other],
             mix_recv.at[item],
             mix_send_sem.at[n],
             mix_recv_sem.at[n],
-            lax.rem(other, sections),
-            other // sections,
+            other // shards,
+            lax.rem(other, shards),
         )
 
     def lat_copy(n):
         other = lax.rem(item + n, group)
         return remote(
             token_latents.at[other // repeat],
-            frame_latents.at[block],
+            frame_latents.at[section, shard],
             lat_send_sem.at[n],
             lat_recv_sem.at[n],
             other // shards,
@@ -220,60 +243,92 @@
 
     start_all(start_copy, shards)
     start_all(half_copy, sections)
-    frame_latents[pl.ds(shard * sections, sections)] = start[shard // repeat]
+    frame_latents[:, shard] = start[shard // repeat]
     token_latents[pl.ds(section * own_frames, own_frames)] = start[:, section]
     for slot in range(slots):
         table[slot] = level_table[levels[slot]]
     wait_all(start_copy, shards)
     wait_all(half_copy, sections)
-    for copy in weight_copies:
-        copy.wait()
+    weight_copies[0].wait()
 
     row_token = lax.rem(lax.broadcasted_iota(jnp.int32, (rows, rows), 0), piece)
     column_token = lax.rem(lax.broadcasted_iota(jnp.int32, (rows, rows), 1), piece)
     same_token = row_token == column_token
+    piece_token = lax.broadcasted_iota(jnp.int32, (piece, lanes), 0)
+    lane_token = lax.broadcasted_iota(jnp.int32, (piece, lanes), 1) // channels
+    own_lanes = piece_token == lane_token
+    high, low = split(embed[...])
+    embed_halves[...] = jnp.concatenate(
+        [high.astype(f32)] * (2 * piece) + [low.astype(f32)] * piece, axis=0
+    ).astype(bf16)
+    high, low = split(final_weight[...])
+    final_halves[...] = jnp.concatenate(
+        [high.astype(f32)] * piece + [low.astype(f32)] * piece, axis=0
+    ).astype(bf16)
+
+    def embedded(packed):
+        spread = jnp.concatenate(
+            [jnp.where(own_lanes, jnp.broadcast_to(row, (piece, lanes)), 0.0) for row in packed],
+            axis=0,
+        )
+        high, low = split(spread)
+        return jnp.dot(
+            jnp.concatenate([high, low, high], axis=1),
+            embed_halves[...],
+            preferred_element_type=f32,
+        )
+
+    def frame_row(n):
+        home = n // piece
+        return (home % sections * shards + home // sections) * piece + n % piece
 
     def step_body(step, carry):
-        whole = jnp.dot(
-            frame_latents[...].reshape(tokens, LANES),
-            embed[...],
-            precision=highest,
-            preferred_element_type=f32,
+        whole = embedded(
+            [frame_latents[n // shards, n % shards] for n in range(group)]
         )
         shift = table[own_slot, 0:1, :]
         scale = 1.0 + table[own_slot, 1:2, :]
         for at in range(0, tokens, slab):
             part = whole[at : at + slab] + pos[at : at + slab, :]
             normed[at : at + slab, :] = (layer_norm(part) * scale + shift).astype(bf16)
-        projected = (
-            jnp.dot(normed[0:tokens, :], spatial_in[...], preferred_element_type=f32)
-            .astype(bf16)
-            .astype(f32)
-        )
-        mixed = attention(
-            projected, heads // repeat, size, gains[0:1, :], gains[1:2, :], None
-        )
-        mix_send[...] = mixed.reshape(group, piece, heads // repeat * size).astype(bf16)
-        start_all(mix_copy, group)
-        mix_recv[item] = mix_send[block]
-
-        token_pos = pos[pl.ds(pl.multiple_of(block * piece, piece), piece), :]
-        base = jnp.dot(
-            token_latents[...].reshape(rows, LANES),
-            embed[...],
-            precision=highest,
-            preferred_element_type=f32,
-        )
+        projected = nt_dot(normed[0:tokens, :], spatial_in[...]).astype(bf16).astype(f32)
+        triples = heads_of(projected, heads // repeat, size, gains[0:1, :], gains[1:2, :])
+        part_width = heads // repeat * size
+        half = group // 2
+        for n in range(2):
+            mixed = attention(triples, n * half * piece, half * piece, None)
+            mix_send[n * half : (n + 1) * half] = mixed.reshape(half, piece, part_width).astype(
+                bf16
+            )
+
+            def send(m, carry):
+                other = n * half + lax.rem(lax.rem(item, half) + m, half)
+
+                @pl.when(other != item)
+                def _():
+                    mix_copy(lax.rem(other - item + group, group)).start()
+
+                return carry
+
+            lax.fori_loop(0, half, send, 0)
+        mix_recv[item] = mix_send[item]
+
+        token_pos = pos[pl.ds(pl.multiple_of(item * piece, piece), piece), :]
+        base = embedded([token_latents[n] for n in range(slots * frames)])
         for n in range(slots * frames):
             hidden[n * piece : (n + 1) * piece, :] = (
                 base[n * piece : (n + 1) * piece] + token_pos
             )
+        @pl.when(step == 0)
+        def _():
+            for copy in weight_copies[1:]:
+                copy.wait()
+
         wait_all(mix_copy, group)
         branch = None
         arrived = mix_recv[...].astype(f32).reshape(
             slots * frames, repeat, piece, heads // repeat * size
         )
-        part_width = heads // repeat * size
         for n in range(repeat):
             part = jnp.dot(
                 arrived[:, n].reshape(rows, part_width).astype(bf16),
@@ -286,7 +341,8 @@
             frame_pos = jnp.concatenate(
                 [
                     jnp.broadcast_to(
-                        pos[slot * frames + n : slot * frames + n + 1, :], (piece, width)
+                        pos[frame_row(slot * frames + n) : frame_row(slot * frames + n) + 1, :],
+                        (piece, width),
                     )
                     for n in range(frames)
                 ],
@@ -301,38 +357,41 @@
             normed[at : at + slab, :] = (
                 layer_norm(part) * (1.0 + table[slot, 4:5, :]) + table[slot, 3:4, :]
             ).astype(bf16)
-        projected = (
-            jnp.dot(normed[0:rows, :], temporal_in[...], preferred_element_type=f32)
-            .astype(bf16)
-            .astype(f32)
-        )
-        mixed = attention(projected, heads, size, gains[2:3, :], gains[3:4, :], same_token)
+        projected = nt_dot(normed[0:rows, :], temporal_in[...]).astype(bf16).astype(f32)
+        triples = heads_of(projected, heads, size, gains[2:3, :], gains[3:4, :])
+        mixed = attention(triples, 0, rows, same_token)
         branch = jnp.dot(mixed.astype(bf16), temporal_out[...], preferred_element_type=f32)
         for slot in range(slots):
             at = slot * slab
             part = hidden[at : at + slab, :] + table[slot, 5:6, :] * branch[at : at + slab]
-            hidden[at : at + slab, :] = (
-                layer_norm(part) * (1.0 + table[slot, 7:8, :]) + table[slot, 6:7, :]
-            )
-        velocity = jnp.dot(
-            hidden[...], final_weight[...], precision=highest, preferred_element_type=f32
-        ).reshape(slots, frames, piece, LANES)
-        before = jnp.float32(0.0)
-        for slot in range(slots):
+            final = layer_norm(part) * (1.0 + table[slot, 7:8, :]) + table[slot, 6:7, :]
+            high, low = split(final)
+            finals[at : at + slab, :] = high
+            finals[rows + at : rows + at + slab, :] = low
+        product = nt_dot(finals[...], final_halves[...])
+        spread = (
+            product[0:rows, 0:lanes] + product[0:rows, lanes : 2 * lanes] + product[rows:, 0:lanes]
+        )
+        for n in range(slots * frames):
+            velocity = jnp.sum(
+                jnp.where(own_lanes, spread[n * piece : (n + 1) * piece], 0.0),
+                axis=0,
+                keepdims=True,
+            )
+            slot = n // frames
             time = (levels[slot].astype(f32) + 1.0) / LEVELS
-            old = token_latents[slot * frames : (slot + 1) * frames]
-            ends[1, slot * frames : (slot + 1) * frames] = old - time * velocity[slot]
+            before = (levels[slot - 1].astype(f32) + 1.0) / LEVELS if slot > 0 else 0.0
+            old = token_latents[n]
+            ends[1, n] = old - time * velocity
             if slot > 0:
-                token_latents[(slot - 1) * frames : slot * frames] = (
-                    old - (time - before) * velocity[slot]
-                )
-            before = time
-        token_latents[(slots - 1) * frames : slots * frames] = noise[step, :, section]
+                token_latents[n - frames] = old - (time - before) * velocity
+        for n in range(frames):
+            token_latents[(slots - 1) * frames + n] = noise[step, n, section]
 
         @pl.when(step < steps - 1)
         def _():
             start_all(lat_copy, group)
-            frame_latents[block] = token_latents[frame]
+            frame_latents[section, shard] = token_latents[frame]
             wait_all(lat_copy, group)
 
         return carry
@@ -370,21 +429,20 @@
     own_frames = blocks * frames
     assert repeat * slots * frames == group and heads % repeat == 0
     assert piece * sections == tokens and own_frames * sections == slots * frames
-    widen = ((0, 0),) * 3 + ((0, LANES - channels),)
-    start = jnp.pad(jnp.transpose(queue_latents, (0, 1, 3, 2)), widen).reshape(
-        own_frames, sections, piece, LANES
-    )
-    noise = jnp.pad(jnp.transpose(fresh_noise, (0, 1, 3, 2)), widen).reshape(
-        steps, frames, sections, piece, LANES
-    )
-    embed = jnp.pad(embed_weight, ((0, LANES - channels), (0, 0)))
-    final = jnp.pad(final_weight, ((0, 0), (0, LANES - channels)))
+    lanes = piece * channels
+
+    def packed(latents):
+        return jnp.transpose(latents, (0, 1, 3, 2)).reshape(-1, frames, sections, 1, lanes)
+
+    start = packed(queue_latents).reshape(own_frames, sections, 1, lanes)
+    noise = packed(fresh_noise)
+    spatial_in, temporal_in, final = spatial_in.T, temporal_in.T, final_weight.T
     part = inner // repeat
     if repeat > 1:
         which = lax.rem(lax.axis_index("space"), repeat)
         spatial_in = lax.dynamic_index_in_dim(
-            spatial_in.reshape(width, 3, repeat, part), which, axis=2, keepdims=False
-        ).reshape(width, 3 * part)
+            spatial_in.reshape(3, repeat, part, width), which, axis=1, keepdims=False
+        ).reshape(3 * part, width)
     rows = max(slots * frames * piece, group * piece)
     cfg = dict(
         sections=sections,
@@ -401,19 +459,22 @@
     dma = pltpu.SemaphoreType.DMA
     out = pl.pallas_call(
         functools.partial(kernel, cfg),
-        out_shape=jax.ShapeDtypeStruct((2, sections, own_frames, piece, LANES), f32),
+        out_shape=jax.ShapeDtypeStruct((2, sections, own_frames, 1, lanes), f32),
         in_specs=[pl.BlockSpec(memory_space=pltpu.SMEM)] + [vmem] * 7 + [anywhere] * 4,
         out_specs=vmem,
         scratch_shapes=[
-            pltpu.VMEM((group, piece, LANES), f32),
-            pltpu.VMEM((slots * frames, piece, LANES), f32),
+            pltpu.VMEM((sections, shards, 1, lanes), f32),
+            pltpu.VMEM((slots * frames, 1, lanes), f32),
             pltpu.VMEM((group, piece, part), bf16),
             pltpu.VMEM((group, piece, part), bf16),
             pltpu.VMEM((slots, level_table.shape[1], width), f32),
             pltpu.VMEM((slots * frames * piece, width), f32),
             pltpu.VMEM((rows, width), bf16),
-            pltpu.VMEM((2, slots * frames, piece, LANES), f32),
-            pltpu.VMEM((2, sections, own_frames, piece, LANES), f32),
+            pltpu.VMEM((2 * slots * frames * piece, width), bf16),
+            pltpu.VMEM((3 * lanes, width), bf16),
+            pltpu.VMEM((2 * lanes, width), bf16),
+            pltpu.VMEM((2, slots * frames, 1, lanes), f32),
+            pltpu.VMEM((2, sections, own_frames, 1, lanes), f32),
             pltpu.VMEM(spatial_in.shape, bf16),
             pltpu.VMEM(spatial_out.shape, bf16),
             pltpu.VMEM(temporal_in.shape, bf16),
@@ -438,8 +499,13 @@
         start,
         noise,
         level_table,
-        jnp.asarray(sincos(max(group * piece, slots * frames), width)),
-        embed,
+        jnp.asarray(
+            sincos(group * piece, width)
+            .reshape(shards, sections, piece, width)
+            .swapaxes(0, 1)
+            .reshape(group * piece, width)
+        ),
+        embed_weight,
         final,
         norm_gains,
         spatial_in,
@@ -447,9 +513,9 @@
         temporal_in,
         temporal_out,
     )
-    ends = jnp.transpose(out[..., :channels], (0, 2, 4, 1, 3)).reshape(
-        2, blocks, frames, channels, tokens
-    )
+    ends = jnp.transpose(
+        out.reshape(2, sections, own_frames, piece, channels), (0, 2, 4, 1, 3)
+    ).reshape(2, blocks, frames, channels, tokens)
     return (ends[0], ends[1])
 
 

time: 86.4 us -> 70.7 us (0.82)
  local copies, waits for them, and re-layouts: 22.2 us -> 5.23 us
  other arithmetic: 0 us -> 1.4 us
    unnamed x7 -> x2, local copies, waits for them, and re-layouts: 17.2 us -> 1.42 us
    pad x3 -> x0, local copies, waits for them, and re-layouts: 3.41 us -> none  [the longest x1 1.81 us: per_device(): embed = jnp.pad(embed_weight, ((0, LANES - channels), (0, 0)))]
    pallas_call x0 -> x1, other arithmetic: none -> 1.4 us  [per_device(): pl.pallas_call(functools.partial(kernel, cfg), out_shape=jax.ShapeDtypeSt...]
    transpose x1 -> x2, local copies, waits for them, and re-layouts: 0.91 us -> 1.78 us  [packed(): jnp.transpose(latents, (0, 1, 3, 2)).reshape(-1, frames, sections, 1, lanes)]
where the time goes in v1:
time: 70.7 us; the launch traced here: 70.3 us
  Pallas kernels  63 us (89%)
  local copies, waits for them, and re-layouts  5.23 us (7%)
  other arithmetic  1.4 us (2%)
    pallas_call x1, Pallas kernels, per_device(): pl.pallas_call(functools.partial(kernel, cfg), out_shape=jax.ShapeDtypeSt...  63 us
    transpose x2, local copies, waits for them, and re-layouts, packed(): jnp.transpose(latents, (0, 1, 3, 2)).reshape(-1, frames, sections, 1, lanes)  1.78 us
    unnamed x2, local copies, waits for them, and re-layouts  1.42 us

profile of v1, /device:TPU:0, one launch (start us, length us, event | category | flops | bytes accessed | tf_op | source)
XLA Modules:
  0.0 70.3 jit_solution(1572598022233429010)
XLA Ops:
  0.6 0.9 %copy.19 = f32[3,2,16,16]{3,2,1,0:T(8,128)S(1)} copy(f32[3,2,16,16]{2,3,1,0:T(8,128)} %bitcast.22) | data formatting | bytes 12288 | tf_op jit(solution)/shard_map/transpose | solution.py:435
  1.5 0.7 reshape.15.noise
  2.2 0.9 %copy.18 = f32[4,2,16,16]{3,2,1,0:T(8,128)S(1)} copy(f32[4,2,16,16]{2,3,1,0:T(8,128)} %bitcast.21) | data formatting | bytes 16384 | tf_op jit(solution)/shard_map/transpose | solution.py:435
  3.1 0.7 reshape_reshape.3.start
  3.8 63.0 %shard_map.131 = f32[2,2,8,1,128]{4,3,2,1,0:T(1,128)} custom-call(s32[8]{0:T(128)} %levels.1, f32[8,2,1,128]{3,2,1,0:T(1,128)} %reshape_reshape.3.start, f32[3,2,2,1,128]{4,3,2,1,0:T(1,128)} %reshape.15.noise, f32[16,8,1152]{2,1,0:T(8,128)} %level_table.1, f32[128,1152]{1,0:T(8,128)} %constant.2.clone.pos, f32[16,1152]{1,0:T(8,128)} %embed.1, ...), custom_call_target="tpu_custom_call" | custom-call | tf_op jit(solution)/shard_map/pallas_call | solution.py:460
  66.9 0.5 broadcast.3
  67.4 1.4 %reduce.3 = f32[2,2,8,128]{3,2,1,0:T(8,128)S(1)} reduce(f32[2,2,8,1,128]{4,3,2,1,0:T(1,128)} %shard_map.131, f32[]{:T(128)} %broadcast.3), dimensions={3}, to_apply=%pallas_call.3.reduce_sub_computation.3 | reduce | bytes 32772 | tf_op jit(solution)/shard_map/pallas_call | solution.py:460
  68.8 0.1 reshape.16
  68.9 0.7 %copy.22 = f32[4,2,16,16]{3,2,1,0:T(8,128)} copy(f32[4,2,16,16]{2,3,1,0:T(8,128)S(1)} %bitcast.19) | data formatting | bytes 16384
  69.6 0.7 %copy.21 = f32[4,2,16,16]{3,2,1,0:T(8,128)} copy(f32[4,2,16,16]{2,3,1,0:T(8,128)S(1)} %bitcast.18) | data formatting | bytes 16384
  (2 shorter events, 0.0 us)

commit v2 on v1

--- a/solution.py
+++ b/solution.py
@@ -27,30 +27,38 @@
     return centered * lax.rsqrt(jnp.mean(centered * centered, axis=-1, keepdims=True) + epsilon)
 
 
-def head_norm(values, gain):
-    return (
-        values * lax.rsqrt(jnp.mean(values * values, axis=-1, keepdims=True) + epsilon) * gain
-    ).astype(bf16)
-
-
 def split(values):
     high = values.astype(bf16)
     return high, (values - high.astype(f32)).astype(bf16)
 
 
-def heads_of(projected, heads, size, query_gain, key_gain):
+def heads_of(projected, heads, size, gain, head_sum, head_spread):
     inner = heads * size
-    result = []
-    for head in range(heads):
-        at = head * size
-        result.append(
-            (
-                head_norm(projected[:, at : at + size], query_gain),
-                head_norm(projected[:, inner + at : inner + at + size], key_gain),
-                projected[:, 2 * inner + at : 2 * inner + at + size].astype(bf16),
-            )
-        )
-    return result
+    rows = projected.shape[0]
+    both = projected[:, : 2 * inner]
+    high, low = split(both * both)
+    sums = jnp.dot(
+        jnp.concatenate([high, low], axis=0),
+        head_sum[: 2 * inner, :],
+        preferred_element_type=f32,
+    )
+    factor = lax.rsqrt((sums[:rows] + sums[rows:]) * (1.0 / size) + epsilon)
+    high, low = split(factor)
+    factor = jnp.dot(
+        jnp.concatenate([high, low], axis=1),
+        head_spread[:, : 2 * inner],
+        preferred_element_type=f32,
+    )
+    both = (both * factor * gain).astype(bf16)
+    values = projected[:, 2 * inner :].astype(bf16)
+    return [
+        (
+            both[:, at : at + size],
+            both[:, inner + at : inner + at + size],
+            values[:, at : at + size],
+        )
+        for at in range(0, inner, size)
+    ]
 
 
 def attention(triples, first, count, mask):
@@ -62,12 +70,12 @@
             (((1,), (1,)), ((), ())),
             preferred_element_type=f32,
         )
-        weights = jnp.exp(scores * (1.0 / math.sqrt(values.shape[1])))
+        weights = jnp.exp2(scores * (math.log2(math.e) / math.sqrt(values.shape[1])))
         if mask is not None:
             weights = jnp.where(mask, weights, 0.0)
         totals = jnp.sum(weights, axis=-1, keepdims=True)
         total = jnp.dot(weights.astype(bf16), values, preferred_element_type=f32)
-        mixed.append(total / totals)
+        mixed.append((total / totals).astype(bf16))
     return jnp.concatenate(mixed, axis=-1)
 
 
@@ -78,18 +86,26 @@
 def kernel(
     cfg,
     levels,
+    queue_latents,
+    fresh_noise,
+    embed,
+    final_weight,
+    gains,
+    level_table_hbm,
+    pos_hbm,
+    spatial_in_hbm,
+    spatial_out_hbm,
+    temporal_in_hbm,
+    temporal_out_hbm,
+    next_queue,
+    denoised,
     start,
     noise,
     level_table,
     pos,
-    embed,
-    final_weight,
-    gains,
-    spatial_in_hbm,
-    spatial_out_hbm,
-    temporal_in_hbm,
-    temporal_out_hbm,
-    out,
+    gain_rows,
+    head_sum,
+    head_spread,
     frame_latents,
     token_latents,
     mix_send,
@@ -137,6 +153,8 @@
         pltpu.make_async_copy(src, dst, weight_sem.at[n])
         for n, (src, dst) in enumerate(
             (
+                (level_table_hbm, level_table),
+                (pos_hbm, pos),
                 (spatial_in_hbm, spatial_in),
                 (spatial_out_hbm, spatial_out),
                 (temporal_in_hbm, temporal_in),
@@ -160,6 +178,34 @@
         return carry
 
     lax.fori_loop(1, group, greet, 0)
+
+    def packed(latents, count):
+        own_tokens = latents.shape[1]
+        wide = sections * lanes
+        token = lax.broadcasted_iota(jnp.int32, (own_tokens, wide), 0)
+        lane = lax.broadcasted_iota(jnp.int32, (own_tokens, wide), 1)
+        spread = jnp.dot(
+            latents,
+            jnp.where(token == lane // channels, 1.0, 0.0),
+            precision=lax.Precision.HIGHEST,
+            preferred_element_type=f32,
+        )
+        channel = lax.broadcasted_iota(jnp.int32, (channels, wide), 0)
+        own = channel == lax.rem(lax.broadcasted_iota(jnp.int32, (channels, wide), 1), channels)
+        return [
+            jnp.sum(
+                jnp.where(own, spread[n * channels : (n + 1) * channels], 0.0),
+                axis=0,
+                keepdims=True,
+            )
+            for n in range(count)
+        ]
+
+    own_tokens = sections * piece
+    lines = packed(queue_latents[...].reshape(own_frames * channels, own_tokens), own_frames)
+    for n, line in enumerate(lines):
+        for t in range(sections):
+            start[n, t] = line[:, t * lanes : (t + 1) * lanes]
     pl.semaphore_wait(barrier, group - 1)
 
     def remote(src, dst, send, recv, to_section, to_shard):
@@ -245,11 +291,30 @@
     start_all(half_copy, sections)
     frame_latents[:, shard] = start[shard // repeat]
     token_latents[pl.ds(section * own_frames, own_frames)] = start[:, section]
-    for slot in range(slots):
-        table[slot] = level_table[levels[slot]]
-    wait_all(start_copy, shards)
-    wait_all(half_copy, sections)
-    weight_copies[0].wait()
+    lines = packed(
+        fresh_noise[...].reshape(steps * frames * channels, own_tokens), steps * frames
+    )
+    for n, line in enumerate(lines):
+        for t in range(sections):
+            noise[n // frames, n % frames, t] = line[:, t * lanes : (t + 1) * lanes]
+    all_heads = 2 * heads * size
+    head_sum[...] = jnp.where(
+        lax.broadcasted_iota(jnp.int32, (all_heads, 128), 0) // size
+        == lax.broadcasted_iota(jnp.int32, (all_heads, 128), 1),
+        1.0,
+        0.0,
+    ).astype(bf16)
+    head_spread[...] = jnp.where(
+        lax.rem(lax.broadcasted_iota(jnp.int32, (256, all_heads), 0), 128)
+        == lax.broadcasted_iota(jnp.int32, (256, all_heads), 1) // size,
+        1.0,
+        0.0,
+    ).astype(bf16)
+    for n, count in enumerate((heads // repeat, heads)):
+        gain_rows[n : n + 1, : 2 * count * size] = jnp.concatenate(
+            [gains[2 * n : 2 * n + 1, :]] * count + [gains[2 * n + 1 : 2 * n + 2, :]] * count,
+            axis=1,
+        )
 
     row_token = lax.rem(lax.broadcasted_iota(jnp.int32, (rows, rows), 0), piece)
     column_token = lax.rem(lax.broadcasted_iota(jnp.int32, (rows, rows), 1), piece)
@@ -266,6 +331,14 @@
         [high.astype(f32)] * piece + [low.astype(f32)] * piece, axis=0
     ).astype(bf16)
 
+    for copy in weight_copies[:2]:
+        copy.wait()
+    for slot in range(slots):
+        table[slot] = level_table[levels[slot]]
+    wait_all(start_copy, shards)
+    wait_all(half_copy, sections)
+    weight_copies[2].wait()
+
     def embedded(packed):
         spread = jnp.concatenate(
             [jnp.where(own_lanes, jnp.broadcast_to(row, (piece, lanes)), 0.0) for row in packed],
@@ -292,13 +365,21 @@
             part = whole[at : at + slab] + pos[at : at + slab, :]
             normed[at : at + slab, :] = (layer_norm(part) * scale + shift).astype(bf16)
         projected = nt_dot(normed[0:tokens, :], spatial_in[...]).astype(bf16).astype(f32)
-        triples = heads_of(projected, heads // repeat, size, gains[0:1, :], gains[1:2, :])
-        part_width = heads // repeat * size
+        part_heads = heads // repeat
+        triples = heads_of(
+            projected,
+            part_heads,
+            size,
+            gain_rows[0:1, : 2 * part_heads * size],
+            head_sum,
+            head_spread,
+        )
+        part_width = part_heads * size
         half = group // 2
         for n in range(2):
             mixed = attention(triples, n * half * piece, half * piece, None)
-            mix_send[n * half : (n + 1) * half] = mixed.reshape(half, piece, part_width).astype(
-                bf16
+            mix_send[n * half : (n + 1) * half] = (
+                mixed.astype(f32).reshape(half, piece, part_width).astype(bf16)
             )
 
             def send(m, carry):
@@ -321,7 +402,7 @@
             )
         @pl.when(step == 0)
         def _():
-            for copy in weight_copies[1:]:
+            for copy in weight_copies[3:]:
                 copy.wait()
 
         wait_all(mix_copy, group)
@@ -358,9 +439,9 @@
                 layer_norm(part) * (1.0 + table[slot, 4:5, :]) + table[slot, 3:4, :]
             ).astype(bf16)
         projected = nt_dot(normed[0:rows, :], temporal_in[...]).astype(bf16).astype(f32)
-        triples = heads_of(projected, heads, size, gains[2:3, :], gains[3:4, :])
+        triples = heads_of(projected, heads, size, gain_rows[1:2, :], head_sum, head_spread)
         mixed = attention(triples, 0, rows, same_token)
-        branch = jnp.dot(mixed.astype(bf16), temporal_out[...], preferred_element_type=f32)
+        branch = jnp.dot(mixed, temporal_out[...], preferred_element_type=f32)
         for slot in range(slots):
             at = slot * slab
             part = hidden[at : at + slab, :] + table[slot, 5:6, :] * branch[at : at + slab]
@@ -401,7 +482,32 @@
     start_all(end_copy, sections)
     landed[:, section] = ends[:, pl.ds(section * own_frames, own_frames)]
     wait_all(end_copy, sections)
-    out[...] = landed[...]
+    spread = jnp.concatenate(
+        [
+            jnp.where(own_lanes, jnp.broadcast_to(landed[k, t, n], (piece, lanes)), 0.0)
+            for k in range(2)
+            for n in range(own_frames)
+            for t in range(sections)
+        ],
+        axis=0,
+    )
+    pick = jnp.where(
+        lax.broadcasted_iota(jnp.int32, (channels, lanes), 0)
+        == lax.rem(lax.broadcasted_iota(jnp.int32, (channels, lanes), 1), channels),
+        1.0,
+        0.0,
+    )
+    result = lax.dot_general(
+        pick,
+        spread,
+        (((1,), (1,)), ((), ())),
+        precision=lax.Precision.HIGHEST,
+        preferred_element_type=f32,
+    )
+    for k, target in enumerate((next_queue, denoised)):
+        for n in range(own_frames):
+            at = (k * own_frames + n) * own_tokens
+            target[n // frames, n % frames] = result[:, at : at + own_tokens]
 
 
 def per_device(
@@ -430,12 +536,6 @@
     assert repeat * slots * frames == group and heads % repeat == 0
     assert piece * sections == tokens and own_frames * sections == slots * frames
     lanes = piece * channels
-
-    def packed(latents):
-        return jnp.transpose(latents, (0, 1, 3, 2)).reshape(-1, frames, sections, 1, lanes)
-
-    start = packed(queue_latents).reshape(own_frames, sections, 1, lanes)
-    noise = packed(fresh_noise)
     spatial_in, temporal_in, final = spatial_in.T, temporal_in.T, final_weight.T
     part = inner // repeat
     if repeat > 1:
@@ -459,10 +559,17 @@
     dma = pltpu.SemaphoreType.DMA
     out = pl.pallas_call(
         functools.partial(kernel, cfg),
-        out_shape=jax.ShapeDtypeStruct((2, sections, own_frames, 1, lanes), f32),
-        in_specs=[pl.BlockSpec(memory_space=pltpu.SMEM)] + [vmem] * 7 + [anywhere] * 4,
-        out_specs=vmem,
+        out_shape=(jax.ShapeDtypeStruct(queue_latents.shape, f32),) * 2,
+        in_specs=[pl.BlockSpec(memory_space=pltpu.SMEM)] + [vmem] * 5 + [anywhere] * 6,
+        out_specs=(vmem, vmem),
         scratch_shapes=[
+            pltpu.VMEM((own_frames, sections, 1, lanes), f32),
+            pltpu.VMEM((steps, frames, sections, 1, lanes), f32),
+            pltpu.VMEM(level_table.shape, f32),
+            pltpu.VMEM((group * piece, width), f32),
+            pltpu.VMEM((2, 2 * inner), f32),
+            pltpu.VMEM((2 * inner, 128), bf16),
+            pltpu.VMEM((256, 2 * inner), bf16),
             pltpu.VMEM((sections, shards, 1, lanes), f32),
             pltpu.VMEM((slots * frames, 1, lanes), f32),
             pltpu.VMEM((group, piece, part), bf16),
@@ -479,7 +586,7 @@
             pltpu.VMEM(spatial_out.shape, bf16),
             pltpu.VMEM(temporal_in.shape, bf16),
             pltpu.VMEM(temporal_out.shape, bf16),
-            dma((4,)),
+            dma((6,)),
             dma((shards,)),
             dma((shards,)),
             dma((sections,)),
@@ -496,8 +603,11 @@
         ),
     )(
         slot_levels,
-        start,
-        noise,
+        queue_latents,
+        fresh_noise,
+        embed_weight,
+        final,
+        norm_gains,
         level_table,
         jnp.asarray(
             sincos(group * piece, width)
@@ -505,18 +615,12 @@
             .swapaxes(0, 1)
             .reshape(group * piece, width)
         ),
-        embed_weight,
-        final,
-        norm_gains,
         spatial_in,
         spatial_out,
         temporal_in,
         temporal_out,
     )
-    ends = jnp.transpose(
-        out.reshape(2, sections, own_frames, piece, channels), (0, 2, 4, 1, 3)
-    ).reshape(2, blocks, frames, channels, tokens)
-    return (ends[0], ends[1])
+    return out
 
 
 def solution(mesh):

time: 70.7 us -> 65.6 us (0.928)
  local copies, waits for them, and re-layouts: 5.23 us -> 2.95 us
  other arithmetic: 1.4 us -> 0 us
  Pallas kernels: 63 us -> 61.7 us
    transpose x2 -> x0, local copies, waits for them, and re-layouts: 1.78 us -> none  [packed(): jnp.transpose(latents, (0, 1, 3, 2)).reshape(-1, frames, sections, 1, lanes)]
    unnamed x2, local copies, waits for them, and re-layouts: 1.42 us -> 2.95 us
    pallas_call x1 -> x0, other arithmetic: 1.4 us -> none  [per_device(): pl.pallas_call(functools.partial(kernel, cfg), out_shape=jax.ShapeDtypeSt...]
    pallas_call x1, Pallas kernels: 63 us -> 61.7 us  [per_device(): pl.pallas_call(functools.partial(kernel, cfg), out_shape=(jax.ShapeDtypeS...]
    reshape x3 -> x0, local copies, waits for them, and re-layouts: 0.79 us -> none  [the longest x1 0.69 us: packed(): jnp.transpose(latents, (0, 1, 3, 2)).reshape(-1, frames, sections, 1, lanes)]
where the time goes in v2:
time: 65.6 us; the launch traced here: 65.3 us
  Pallas kernels  61.7 us (94%)
  local copies, waits for them, and re-layouts  2.95 us (4%)
    pallas_call x1, Pallas kernels, per_device(): pl.pallas_call(functools.partial(kernel, cfg), out_shape=(jax.ShapeDtypeS...  61.7 us
    unnamed x2, local copies, waits for them, and re-layouts  2.95 us

profile of v2, /device:TPU:0, one launch (start us, length us, event | category | flops | bytes accessed | tf_op | source)
XLA Modules:
  0.0 65.3 jit_solution(9623270175016328663)
XLA Ops:
  0.6 61.7 %shard_map.131 = (f32[4,2,16,16]{3,2,1,0:T(8,128)}, f32[4,2,16,16]{3,2,1,0:T(8,128)}) custom-call(s32[8]{0:T(128)} %levels.1, f32[4,2,16,16]{3,2,1,0:T(8,128)} %queue_latents.1, f32[3,2,16,16]{3,2,1,0:T(8,128)} %fresh_noise.1, f32[16,1152]{1,0:T(8,128)} %embed.1, f32[16,1152]{1,0:T(8,128)} %bitcast.5, f32[4,72]{1,0:T(4,128)} %gains.1, ...), custom_call_target="tpu_custom_call" | custom-call | tf_op jit(solution)/shard_map/pallas_call | solution.py:560
  62.4 1.5 %copy.16 = f32[4,2,16,16]{3,2,1,0:T(8,128)} copy(f32[4,2,16,16]{3,2,1,0:T(8,128)} %get-tuple-element.4) | data formatting | bytes 16384
  63.9 1.5 %copy.17 = f32[4,2,16,16]{3,2,1,0:T(8,128)} copy(f32[4,2,16,16]{3,2,1,0:T(8,128)} %get-tuple-element.5) | data formatting | bytes 16384

commit v3 on v2

--- a/solution.py
+++ b/solution.py
@@ -97,8 +97,7 @@
     spatial_out_hbm,
     temporal_in_hbm,
     temporal_out_hbm,
-    next_queue,
-    denoised,
+    out,
     start,
     noise,
     level_table,
@@ -482,6 +481,16 @@
     start_all(end_copy, sections)
     landed[:, section] = ends[:, pl.ds(section * own_frames, own_frames)]
     wait_all(end_copy, sections)
+    out[...] = landed[...]
+
+
+def unpack(frames, landed, next_queue, denoised):
+    _, sections, own_frames, _, lanes = landed.shape
+    channels = next_queue.shape[2]
+    piece = lanes // channels
+    own_tokens = sections * piece
+    piece_token = lax.broadcasted_iota(jnp.int32, (piece, lanes), 0)
+    own_lanes = piece_token == lax.broadcasted_iota(jnp.int32, (piece, lanes), 1) // channels
     spread = jnp.concatenate(
         [
             jnp.where(own_lanes, jnp.broadcast_to(landed[k, t, n], (piece, lanes)), 0.0)
@@ -557,11 +566,11 @@
     )
     vmem, anywhere = pl.BlockSpec(memory_space=pltpu.VMEM), pl.BlockSpec(memory_space=pl.ANY)
     dma = pltpu.SemaphoreType.DMA
-    out = pl.pallas_call(
+    landed = pl.pallas_call(
         functools.partial(kernel, cfg),
-        out_shape=(jax.ShapeDtypeStruct(queue_latents.shape, f32),) * 2,
+        out_shape=jax.ShapeDtypeStruct((2, sections, own_frames, 1, lanes), f32),
         in_specs=[pl.BlockSpec(memory_space=pltpu.SMEM)] + [vmem] * 5 + [anywhere] * 6,
-        out_specs=(vmem, vmem),
+        out_specs=vmem,
         scratch_shapes=[
             pltpu.VMEM((own_frames, sections, 1, lanes), f32),
             pltpu.VMEM((steps, frames, sections, 1, lanes), f32),
@@ -620,7 +629,12 @@
         temporal_in,
         temporal_out,
     )
-    return out
+    return pl.pallas_call(
+        functools.partial(unpack, frames),
+        out_shape=(jax.ShapeDtypeStruct(queue_latents.shape, f32),) * 2,
+        in_specs=[vmem],
+        out_specs=(vmem, vmem),
+    )(landed)
 
 
 def solution(mesh):

time: 65.6 us -> 63.9 us (0.974)
  local copies, waits for them, and re-layouts: 2.95 us -> 0 us
  Pallas kernels: 61.7 us -> 63.1 us
    unnamed x2 -> x0, local copies, waits for them, and re-layouts: 2.95 us -> none
    pallas_call x1 -> x2, Pallas kernels: 61.7 us -> 63.1 us  [the longest x1 61.4 us: per_device(): pl.pallas_call(functools.partial(kernel, cfg), out_shape=jax.ShapeDtypeSt...]
where the time goes in v3:
time: 63.9 us; the launch traced here: 63.7 us
  Pallas kernels  63.1 us (99%)
  between operations  0.64 us (1%)
    pallas_call x1, Pallas kernels, per_device(): pl.pallas_call(functools.partial(kernel, cfg), out_shape=jax.ShapeDtypeSt...  61.4 us
    pallas_call x1, Pallas kernels, per_device(): pl.pallas_call(functools.partial(unpack, frames), out_shape=(jax.ShapeDty...  1.69 us

profile of v3, /device:TPU:0, one launch (start us, length us, event | category | flops | bytes accessed | tf_op | source)
XLA Modules:
  0.0 63.7 jit_solution(15392930707050376077)
XLA Ops:
  0.6 61.4 %shard_map.131.landed = f32[2,2,8,1,128]{4,3,2,1,0:T(1,128)} custom-call(s32[8]{0:T(128)} %levels.1, f32[4,2,16,16]{3,2,1,0:T(8,128)} %queue_latents.1, f32[3,2,16,16]{3,2,1,0:T(8,128)} %fresh_noise.1, f32[16,1152]{1,0:T(8,128)} %embed.1, f32[16,1152]{1,0:T(8,128)} %bitcast.5, f32[4,72]{1,0:T(4,128)} %gains.1, f32[16,8,1152]{2,1,0:T(8,128)} %level_table_hbm.1, ...), custom_call_target="tpu_custom_call" | custom-call | tf_op jit(solution)/shard_map/pallas_call | solution.py:569
  62.0 1.7 %shard_map.132 = (f32[4,2,16,16]{3,2,1,0:T(8,128)}, f32[4,2,16,16]{3,2,1,0:T(8,128)}) custom-call(f32[2,2,8,1,128]{4,3,2,1,0:T(1,128)} %shard_map.131.landed), custom_call_target="tpu_custom_call" | custom-call | tf_op jit(solution)/shard_map/pallas_call | solution.py:632
